TPU v7x, 256 devices: a whole 4x4x8 slice. The times are simulated.
256 devices in a mesh: blk: 8 (over x, core), sub: 32 (over z, y).
Axes of the slice: x: 4, y: 4, z: 8, core: 2. Of those that a mesh axis runs over, the one named last changes fastest.
Arguments:
- user_factors: float32 [262144, 1024], P(('blk', 'sub')), may hold values from -6 to 6
- item_factors: bfloat16 [2048, 1024], P(('blk', 'sub')), may hold values from -6 to 6
- ratings: bfloat16 [262144, 1024], P(('blk', 'sub')), may hold values from -6 to 6
- presence: int32 [2048, 8, 2], P(('blk', 'sub')), may hold values 0 or 1
- visit_order: int32 [8], replicated, may hold values from 0 to 7, each once
Outputs:
- users_out: float32 [262144, 1024], P(('blk', 'sub'))
- items_out: bfloat16 [2048, 1024], P(('blk', 'sub'))
All inputs are finite; a program needn't handle non-finite values. No bound on the sum of `presence` on one device may be relied on, other than what follows from the above.
Results may differ from a plain program's by a relative error of at most 0.017.
Values may be sent and summed in bfloat16 or wider, within the bound.
No kernel may reach another device: no remote copies, remote signals or barrier semaphores. Data moves between devices by JAX's collectives and lax.ppermute only.
A program may use at most 64 MiB of HBM per device.

v0:
```python
import math
import jax
import jax.numpy as jnp
from jax import lax
from jax.sharding import PartitionSpec as P

R = 1024
BS = 256
TICKS = 4
learn_users = 0.5
decay_weight = 0.05


def passed_along(block, axis, distance):
    devices = range(lax.axis_size(axis))
    route = [((i - distance) % len(devices), i) for i in devices]
    return lax.ppermute(block, axis, route)


def on_device(user_factors, item_factors, ratings, presence, visit_order):
    scale = R ** (-0.5)
    group_count = lax.axis_size("blk")
    group = lax.axis_index("blk")
    part_index = lax.axis_index("sub")
    part_rows = item_factors.shape[0]
    local_users = user_factors.shape[0]
    group_users = lax.axis_size("sub") * local_users
    step_items = 0.9 * R / (math.sqrt(group_users) + math.sqrt(R)) ** 2
    tile_users = presence.shape[0]
    tile_items = presence.shape[2]
    users_now = user_factors
    item_block = lax.all_gather(item_factors, "sub", axis=0, tiled=True)
    for step_index in range(TICKS):
        position = jnp.mod(group - step_index, group_count)
        ident = jnp.sum(jnp.where(jnp.arange(group_count) == position, visit_order, 0))
        picked = lax.dynamic_index_in_dim(presence, ident, 1, keepdims=False)
        present = jnp.broadcast_to(
            picked[:, None, :, None],
            (tile_users, local_users // tile_users, tile_items, BS // tile_items),
        )
        present = present.reshape(local_users, BS).astype(jnp.float32)
        users_half = users_now.astype(jnp.bfloat16)
        predicted = (
            lax.dot_general(
                users_half, item_block, (((1,), (1,)), ((), ())), preferred_element_type=jnp.float32
            )
            * scale
        )
        targets = ratings[:, step_index * BS : (step_index + 1) * BS].astype(jnp.float32)
        residual = (present * (predicted - targets)).astype(jnp.bfloat16)
        user_grad = jnp.dot(residual, item_block, preferred_element_type=jnp.float32) * scale
        item_part = (
            lax.dot_general(
                residual, users_half, (((0,), (0,)), ((), ())), preferred_element_type=jnp.float32
            )
            * scale
        ).astype(jnp.bfloat16)
        users_now = users_now - learn_users * (user_grad + decay_weight * users_now)
        item_grad = lax.psum(item_part, "sub").astype(jnp.float32)
        block_wide = item_block.astype(jnp.float32)
        updated = (block_wide - step_items * (item_grad + decay_weight * block_wide)).astype(
            jnp.bfloat16
        )
        item_block = passed_along(updated, "blk", 1)
    held_part = lax.dynamic_slice_in_dim(item_block, part_index * part_rows, part_rows, 0)
    return (users_now, held_part)


def solution(mesh):
    in_specs = (
        P(("blk", "sub"), None),
        P(("blk", "sub"), None),
        P(("blk", "sub"), None),
        P(("blk", "sub"), None, None),
        P(),
    )
    out_specs = (P(("blk", "sub"), None), P(("blk", "sub"), None))
    return jax.shard_map(
        on_device, mesh=mesh, in_specs=in_specs, out_specs=out_specs, check_vma=False
    )
```

profile of v0, /device:TPU:1, one launch (start us, length us, event | category | flops | bytes accessed | tf_op | source)
XLA Modules:
  0.0 718.2 jit_solution(10500018908168411886)
XLA Ops:
  7.2 0.0 all-reduce.5.cloned.1.call-start
  7.3 1.4 fusion.39
  16.3 0.9 constant_dynamic-slice_fusion.1
  17.3 0.1 copy.23
  17.4 0.1 copy.16
  17.5 42.6 %all_gather.3 = bf16[256,1024]{1,0:T(8,128)(2,1)S(1)} all-gather(bf16[8,1024]{1,0:T(8,128)(2,1)} %param.6), channel_id=1, replica_groups=mesh['blk'=8,'sub'=32] {'sub'}, dimensions={0}, use_global_device_ids=true | all-gather | bytes 540672 | tf_op jit(solution)/shard_map/all_gather | solution.py:32
  60.1 0.3 broadcast_in_dim.16
  60.4 3.1 fusion.8
  63.5 1.5 fusion.9
  65.0 0.0 all-reduce.7.cloned.1.call-start
  65.1 0.1 copy.24
  65.2 153.3 %all-reduce.5.cloned.1.call-done = bf16[256,1024]{1,0:T(8,128)(2,1)} async-done(((bf16[256,1024]{1,0:T(8,128)(2,1)}), bf16[256,1024]{1,0:T(8,128)(2,1)}) %all-reduce.5.cloned.1.call-update) | async-done | bytes 524304 | tf_op jit(solution)/shard_map/psum | solution.py:59
  218.5 1.3 fusion.18
  219.8 6.3 collective-permute-start
  226.0 0.1 copy.18
  226.1 3.1 multiply_subtract_fusion.3
  229.2 2.9 collective-permute-done
  232.1 0.3 broadcast_in_dim.17
  232.5 1.8 fusion.10
  234.3 1.6 fusion.11
  235.9 0.0 all-reduce.9.cloned.1.call-start
  236.0 0.1 copy.25
  236.0 142.1 %all-reduce.7.cloned.1.call-done = bf16[256,1024]{1,0:T(8,128)(2,1)} async-done(((bf16[256,1024]{1,0:T(8,128)(2,1)}), bf16[256,1024]{1,0:T(8,128)(2,1)}) %all-reduce.7.cloned.1.call-update) | async-done | bytes 524304 | tf_op jit(solution)/shard_map/psum | solution.py:59
  378.1 1.3 fusion.21
  379.4 6.3 collective-permute-start.1
  385.7 0.1 copy.20
  385.8 3.1 multiply_subtract_fusion.2
  388.9 2.9 collective-permute-done.1
  391.8 0.3 broadcast_in_dim.34
  392.1 1.8 fusion.12
  394.0 1.5 fusion.13
  395.6 0.2 all-reduce.11.cloned.1.call-start
  395.8 0.1 copy.26
  395.9 141.9 %all-reduce.9.cloned.1.call-done = bf16[256,1024]{1,0:T(8,128)(2,1)} async-done(((bf16[256,1024]{1,0:T(8,128)(2,1)}), bf16[256,1024]{1,0:T(8,128)(2,1)}) %all-reduce.9.cloned.1.call-update) | async-done | bytes 524304 | tf_op jit(solution)/shard_map/psum | solution.py:59
  537.8 1.3 fusion.24
  539.0 6.3 collective-permute-start.2
  545.3 0.1 copy.22
  545.4 3.1 multiply_subtract_fusion.1
  548.5 2.9 collective-permute-done.2
  551.4 0.3 broadcast_in_dim.35
  551.8 1.8 fusion.14
  553.6 1.6 fusion.15
  555.2 142.3 %all-reduce.11.cloned.1.call-done = bf16[256,1024]{1,0:T(8,128)(2,1)} async-done(((bf16[256,1024]{1,0:T(8,128)(2,1)}), bf16[256,1024]{1,0:T(8,128)(2,1)}) %all-reduce.11.cloned.1.call-update) | async-done | bytes 524304 | tf_op jit(solution)/shard_map/psum | solution.py:59
  697.4 1.3 fusion.27
  698.7 6.3 collective-permute-start.3
  705.0 5.1 multiply_subtract_fusion
  710.1 1.0 collective-permute-done.3
  711.1 0.6 constant_dynamic-slice_fusion
  (16 shorter events, 0.1 us)
Async XLA Ops:
  7.2 211.3 %all-reduce.5.cloned.1.call-start = ((), (), s32[]{:S(2)}) async-start(), calls=%async_computation | async-start | bytes 1048576 | tf_op jit(solution)/shard_map/psum | solution.py:59
  17.4 46.0 %copy-start.3 = (f32[1024,1024]{1,0:T(8,128)S(1)}, f32[1024,1024]{1,0:T(8,128)}, u32[]{:S(2)}) copy-start(f32[1024,1024]{1,0:T(8,128)} %param.5) | copy-start | bytes 12582916
  65.0 313.1 %all-reduce.7.cloned.1.call-start = ((), (), s32[]{:S(2)}) async-start(), calls=%async_computation.1 | async-start | bytes 1048576 | tf_op jit(solution)/shard_map/psum | solution.py:59
  219.8 12.4 %collective-permute-start = (bf16[256,1024]{1,0:T(8,128)(2,1)S(1)}, bf16[256,1024]{1,0:T(8,128)(2,1)S(1)}, u32[]{:S(2)}, u32[]{:S(2)}) collective-permute-start(bf16[256,1024]{1,0:T(8,128)(2,1)S(1)} %fusion.18), channel_id=1, source_target_pairs={{224,0},{0,32},{32,64},{64,96},{96,128},{128,160},{160,192},{192,2... | collective-permute-start | bytes 1572872 | tf_op jit(solution)/shard_map/ppermute | solution.py:17
  229.2 5.1 copy-start.2
  235.9 301.9 %all-reduce.9.cloned.1.call-start = ((), (), s32[]{:S(2)}) async-start(), calls=%async_computation.2 | async-start | bytes 1048576 | tf_op jit(solution)/shard_map/psum | solution.py:59
  379.4 12.4 %collective-permute-start.1 = (bf16[256,1024]{1,0:T(8,128)(2,1)S(1)}, bf16[256,1024]{1,0:T(8,128)(2,1)S(1)}, u32[]{:S(2)}, u32[]{:S(2)}) collective-permute-start(bf16[256,1024]{1,0:T(8,128)(2,1)S(1)} %fusion.21), channel_id=1, source_target_pairs={{224,0},{0,32},{32,64},{64,96},{96,128},{128,160},{160,192},{192,2... | collective-permute-start | bytes 1572872 | tf_op jit(solution)/shard_map/ppermute | solution.py:17
  388.9 5.1 copy-start.1
  395.6 301.9 %all-reduce.11.cloned.1.call-start = ((), (), s32[]{:S(2)}) async-start(), calls=%async_computation.3 | async-start | bytes 1048576 | tf_op jit(solution)/shard_map/psum | solution.py:59
  539.0 12.4 %collective-permute-start.2 = (bf16[256,1024]{1,0:T(8,128)(2,1)S(1)}, bf16[256,1024]{1,0:T(8,128)(2,1)S(1)}, u32[]{:S(2)}, u32[]{:S(2)}) collective-permute-start(bf16[256,1024]{1,0:T(8,128)(2,1)S(1)} %fusion.24), channel_id=1, source_target_pairs={{224,0},{0,32},{32,64},{64,96},{96,128},{128,160},{160,192},{192,2... | collective-permute-start | bytes 1572872 | tf_op jit(solution)/shard_map/ppermute | solution.py:17
  548.5 5.1 copy-start
  698.7 12.4 %collective-permute-start.3 = (bf16[256,1024]{1,0:T(8,128)(2,1)S(1)}, bf16[256,1024]{1,0:T(8,128)(2,1)S(1)}, u32[]{:S(2)}, u32[]{:S(2)}) collective-permute-start(bf16[256,1024]{1,0:T(8,128)(2,1)S(1)} %fusion.27), channel_id=1, source_target_pairs={{224,0},{0,32},{32,64},{64,96},{96,128},{128,160},{160,192},{192,2... | collective-permute-start | bytes 1572872 | tf_op jit(solution)/shard_map/ppermute | solution.py:17
Sparse Core Ops, SparseCore 0:
  65.2 153.2 all-reduce.4
  236.0 142.0 all-reduce.6
  395.7 142.0 all-reduce.8
  555.3 142.0 all-reduce.10
where the time goes:
time: 719 us; the launch traced here: 718 us
  waiting for transfers between devices  589 us (82%)
  blocking collectives  42.6 us (6%)
  matrix products  29.2 us (4%)
  starting transfers between devices  25.4 us (4%)
  between operations  21.6 us (3%)
    psum x4, waiting for transfers between devices, on_device(): item_grad = lax.psum(item_part, 'sub').astype(jnp.float32)  580 us
    all_gather x1, blocking collectives, on_device(): item_block = lax.all_gather(item_factors, 'sub', axis=0, tiled=True)  42.6 us
    ppermute x4, starting transfers between devices, passed_along(): return lax.ppermute(block, axis, route)  25 us
    dot_general x4, matrix products, on_device(): jnp.dot(residual, item_block, preferred_element_type=jnp.float32) * scale  14.4 us
  transfers between devices with their start and end apart: 8, of which 8 were waited for; matrix products, arithmetic and copies ran while one was open for 2% of the time, Pallas kernels for 0%

commit v1 on v0

--- a/solution.py
+++ b/solution.py
@@ -29,7 +29,9 @@
     tile_users = presence.shape[0]
     tile_items = presence.shape[2]
     users_now = user_factors
-    item_block = lax.all_gather(item_factors, "sub", axis=0, tiled=True)
+    item_block = jnp.concatenate(
+        lax.all_to_all(jnp.stack([item_factors] * lax.axis_size("sub")), "sub", 0, 0), axis=0
+    )
     for step_index in range(TICKS):
         position = jnp.mod(group - step_index, group_count)
         ident = jnp.sum(jnp.where(jnp.arange(group_count) == position, visit_order, 0))

time: 719 us -> 685 us (0.953)
  blocking collectives: 42.6 us -> 0 us
  starting transfers between devices: 25.4 us -> 37.4 us
    all_gather x1 -> x0, blocking collectives: 42.6 us -> none  [on_device(): item_block = lax.all_gather(item_factors, 'sub', axis=0, tiled=True)]
    all_to_all x0 -> x1, starting transfers between devices: none -> 12 us  [on_device(): lax.all_to_all(jnp.stack([item_factors] * lax.axis_size('sub')), 'sub', 0...]
    psum x4, waiting for transfers between devices: 580 us -> 569 us  [on_device(): item_grad = lax.psum(item_part, 'sub').astype(jnp.float32)]
  transfers between devices with their start and end apart: 8 -> 9, of which waited for: 8 -> 9; matrix products, arithmetic and copies ran while one was open for 2% -> 3% of each run, Pallas kernels for 0% -> 0%
where the time goes in v1:
time: 685 us; the launch traced here: 684 us
  waiting for transfers between devices  585 us (85%)
  starting transfers between devices  37.4 us (5%)
  matrix products  29.4 us (4%)
  between operations  21.4 us (3%)
    psum x4, waiting for transfers between devices, on_device(): item_grad = lax.psum(item_part, 'sub').astype(jnp.float32)  569 us
    ppermute x4, starting transfers between devices, passed_along(): return lax.ppermute(block, axis, route)  25 us
    dot_general x4, matrix products, on_device(): jnp.dot(residual, item_block, preferred_element_type=jnp.float32) * scale  14.4 us
  transfers between devices with their start and end apart: 9, of which 9 were waited for; matrix products, arithmetic and copies ran while one was open for 3% of the time, Pallas kernels for 0%

profile of v1, /device:TPU:1, one launch (start us, length us, event | category | flops | bytes accessed | tf_op | source)
XLA Modules:
  0.0 684.4 jit_solution(2204255272230044404)
XLA Ops:
  7.2 1.6 stack.2
  8.7 12.0 %all-to-all-start = ((bf16[32,8,1024]{2,1,0:T(8,128)(2,1)}), bf16[32,8,1024]{2,1,0:T(8,128)(2,1)S(1)}, u32[]{:S(2)}, u32[]{:S(2)}) async-start(bf16[32,8,1024]{2,1,0:T(8,128)(2,1)} %stack.2), calls=%async_computation | async-start | bytes 1048576 | tf_op jit(solution)/shard_map/all_to_all | solution.py:33
  20.9 1.4 fusion.41
  29.7 0.9 constant_dynamic-slice_fusion.1
  30.6 0.1 copy.23
  30.7 0.1 copy.16
  30.8 6.2 all-to-all-done
  37.1 0.3 broadcast_in_dim.16
  37.4 3.2 fusion.8
  40.7 1.5 fusion.9
  42.2 0.0 all-reduce.7.cloned.1.call-start
  42.3 0.1 copy.24
  42.4 142.2 %all-reduce.5.cloned.1.call-done = bf16[256,1024]{1,0:T(8,128)(2,1)} async-done(((bf16[256,1024]{1,0:T(8,128)(2,1)}), bf16[256,1024]{1,0:T(8,128)(2,1)}) %all-reduce.5.cloned.1.call-update) | async-done | bytes 524304 | tf_op jit(solution)/shard_map/psum | solution.py:61
  184.6 1.3 fusion.18
  185.9 6.3 collective-permute-start
  192.1 0.1 copy.18
  192.2 3.1 multiply_subtract_fusion.3
  195.3 2.9 collective-permute-done
  198.3 0.3 broadcast_in_dim.17
  198.6 1.8 fusion.10
  200.5 1.6 fusion.11
  202.1 0.1 copy.25
  202.2 142.1 %all-reduce.7.cloned.1.call-done = bf16[256,1024]{1,0:T(8,128)(2,1)} async-done(((bf16[256,1024]{1,0:T(8,128)(2,1)}), bf16[256,1024]{1,0:T(8,128)(2,1)}) %all-reduce.7.cloned.1.call-update) | async-done | bytes 524304 | tf_op jit(solution)/shard_map/psum | solution.py:61
  344.3 1.3 fusion.21
  345.5 6.3 collective-permute-start.1
  351.8 0.1 copy.20
  351.9 3.1 multiply_subtract_fusion.2
  355.0 2.9 collective-permute-done.1
  357.9 0.3 broadcast_in_dim.34
  358.3 1.8 fusion.12
  360.1 1.5 fusion.13
  361.7 0.2 all-reduce.11.cloned.1.call-start
  361.9 0.1 copy.26
  362.0 142.0 %all-reduce.9.cloned.1.call-done = bf16[256,1024]{1,0:T(8,128)(2,1)} async-done(((bf16[256,1024]{1,0:T(8,128)(2,1)}), bf16[256,1024]{1,0:T(8,128)(2,1)}) %all-reduce.9.cloned.1.call-update) | async-done | bytes 524304 | tf_op jit(solution)/shard_map/psum | solution.py:61
  504.0 1.3 fusion.24
  505.3 6.3 collective-permute-start.2
  511.5 0.1 copy.22
  511.6 3.1 multiply_subtract_fusion.1
  514.7 2.9 collective-permute-done.2
  517.6 0.3 broadcast_in_dim.35
  518.0 1.8 fusion.14
  519.8 1.6 fusion.15
  521.4 142.2 %all-reduce.11.cloned.1.call-done = bf16[256,1024]{1,0:T(8,128)(2,1)} async-done(((bf16[256,1024]{1,0:T(8,128)(2,1)}), bf16[256,1024]{1,0:T(8,128)(2,1)}) %all-reduce.11.cloned.1.call-update) | async-done | bytes 524304 | tf_op jit(solution)/shard_map/psum | solution.py:61
  663.6 1.3 fusion.27
  664.9 6.3 collective-permute-start.3
  671.2 5.1 multiply_subtract_fusion
  676.3 1.0 collective-permute-done.3
  677.3 0.6 constant_dynamic-slice_fusion
  (18 shorter events, 0.2 us)
Async XLA Ops:
  8.7 28.3 %all-to-all-start = ((bf16[32,8,1024]{2,1,0:T(8,128)(2,1)}), bf16[32,8,1024]{2,1,0:T(8,128)(2,1)S(1)}, u32[]{:S(2)}, u32[]{:S(2)}) async-start(bf16[32,8,1024]{2,1,0:T(8,128)(2,1)} %stack.2), calls=%async_computation | async-start | bytes 1048576 | tf_op jit(solution)/shard_map/all_to_all | solution.py:33
  20.8 163.8 %all-reduce.5.cloned.1.call-start = ((), (), s32[]{:S(2)}) async-start(), calls=%async_computation.1 | async-start | bytes 1048576 | tf_op jit(solution)/shard_map/psum | solution.py:61
  37.1 3.6 copy-start.3
  42.2 302.0 %all-reduce.7.cloned.1.call-start = ((), (), s32[]{:S(2)}) async-start(), calls=%async_computation.2 | async-start | bytes 1048576 | tf_op jit(solution)/shard_map/psum | solution.py:61
  185.9 12.4 %collective-permute-start = (bf16[256,1024]{1,0:T(8,128)(2,1)S(1)}, bf16[256,1024]{1,0:T(8,128)(2,1)S(1)}, u32[]{:S(2)}, u32[]{:S(2)}) collective-permute-start(bf16[256,1024]{1,0:T(8,128)(2,1)S(1)} %fusion.18), channel_id=1, source_target_pairs={{224,0},{0,32},{32,64},{64,96},{96,128},{128,160},{160,192},{192,2... | collective-permute-start | bytes 1572872 | tf_op jit(solution)/shard_map/ppermute | solution.py:17
  195.3 5.1 copy-start.2
  202.0 302.0 %all-reduce.9.cloned.1.call-start = ((), (), s32[]{:S(2)}) async-start(), calls=%async_computation.3 | async-start | bytes 1048576 | tf_op jit(solution)/shard_map/psum | solution.py:61
  345.5 12.4 %collective-permute-start.1 = (bf16[256,1024]{1,0:T(8,128)(2,1)S(1)}, bf16[256,1024]{1,0:T(8,128)(2,1)S(1)}, u32[]{:S(2)}, u32[]{:S(2)}) collective-permute-start(bf16[256,1024]{1,0:T(8,128)(2,1)S(1)} %fusion.21), channel_id=1, source_target_pairs={{224,0},{0,32},{32,64},{64,96},{96,128},{128,160},{160,192},{192,2... | collective-permute-start | bytes 1572872 | tf_op jit(solution)/shard_map/ppermute | solution.py:17
  355.0 5.1 copy-start.1
  361.7 302.0 %all-reduce.11.cloned.1.call-start = ((), (), s32[]{:S(2)}) async-start(), calls=%async_computation.4 | async-start | bytes 1048576 | tf_op jit(solution)/shard_map/psum | solution.py:61
  505.3 12.4 %collective-permute-start.2 = (bf16[256,1024]{1,0:T(8,128)(2,1)S(1)}, bf16[256,1024]{1,0:T(8,128)(2,1)S(1)}, u32[]{:S(2)}, u32[]{:S(2)}) collective-permute-start(bf16[256,1024]{1,0:T(8,128)(2,1)S(1)} %fusion.24), channel_id=1, source_target_pairs={{224,0},{0,32},{32,64},{64,96},{96,128},{128,160},{160,192},{192,2... | collective-permute-start | bytes 1572872 | tf_op jit(solution)/shard_map/ppermute | solution.py:17
  514.7 5.1 copy-start
  664.9 12.4 %collective-permute-start.3 = (bf16[256,1024]{1,0:T(8,128)(2,1)S(1)}, bf16[256,1024]{1,0:T(8,128)(2,1)S(1)}, u32[]{:S(2)}, u32[]{:S(2)}) collective-permute-start(bf16[256,1024]{1,0:T(8,128)(2,1)S(1)} %fusion.27), channel_id=1, source_target_pairs={{224,0},{0,32},{32,64},{64,96},{96,128},{128,160},{160,192},{192,2... | collective-permute-start | bytes 1572872 | tf_op jit(solution)/shard_map/ppermute | solution.py:17
Sparse Core Ops, SparseCore 0:
  42.3 142.2 all-reduce.4
  202.2 142.0 all-reduce.6
  361.8 142.1 all-reduce.8
  521.5 142.0 all-reduce.10
